TPU v7x, 512 devices: a whole 4x8x8 slice. The times are simulated.
512 devices in a mesh: ctx: 128 (over y, z, core), head: 4 (over x).
Axes of the slice: x: 4, y: 8, z: 8, core: 2. Of those that a mesh axis runs over, the one named last changes fastest.
Arguments:
- queries: bfloat16 [16384, 64, 576], P('ctx', 'head'), may hold values from -100 to 100
- latent_cache: bfloat16 [256, 36864], P('ctx'), may hold values from -6 to 6
- selected: int32 [256, 8], P('ctx'), may hold values from -1 to 255, as said below
- value_weight: bfloat16 [64, 512, 128], P('head'), may hold values from -0.25 to 0.25
Outputs:
- attended: bfloat16 [16384, 8192], P(('ctx', 'head'))
Inputs may be any that keep to these rules, and one draw needn't show every extreme that they name: `selected`: row b lists distinct key blocks: its first entry is b itself, the others lie below b; where b + 1 < 8 the row holds all of 0 to b and its remaining slots are -1.
All inputs are finite; a program needn't handle non-finite values.
Results may differ from a plain program's by a relative error of at most 0.011.
Values may be sent and summed in bfloat16 or wider, within the bound.
No kernel may reach another device: no remote copies, remote signals or barrier semaphores. Data moves between devices by JAX's collectives and lax.ppermute only.
A program may use at most 64 MiB of HBM per device.

v0:
```python
import jax
import jax.numpy as jnp
from jax import lax
from jax.sharding import PartitionSpec as P

DC = 512
DR = 64
DV = 128
KBLK = 64
SEL = 8


def attend_block(query_rows, key_rows, chosen_ids, block_index, value_weight):
    score_scale = (DV + DR) ** (-0.5)
    offsets = jnp.arange(KBLK, dtype=jnp.int32)
    valid_slot = chosen_ids >= 0
    clipped = jnp.maximum(chosen_ids, 0)
    key_place = (clipped[:, None] * KBLK + offsets[None, :]).reshape(-1)
    key_valid = jnp.repeat(valid_slot, KBLK)
    query_place = block_index * KBLK + offsets
    scores = (
        jnp.einsum("qhc,kc->hqk", query_rows, key_rows, preferred_element_type=jnp.float32)
        * score_scale
    )
    allowed = key_valid[None, None, :] & (key_place[None, None, :] <= query_place[None, :, None])
    scores = jnp.where(allowed, scores, -1e30)
    largest = jnp.max(scores, axis=2, keepdims=True)
    powered = jnp.exp(scores - largest)
    weights = (powered / jnp.sum(powered, axis=2, keepdims=True)).astype(jnp.bfloat16)
    mixed_latent = jnp.einsum(
        "hqk,kc->qhc", weights, key_rows[:, :DC], preferred_element_type=jnp.float32
    ).astype(jnp.bfloat16)
    expanded = jnp.einsum(
        "qhc,hcv->qhv", mixed_latent, value_weight, preferred_element_type=jnp.float32
    )
    return expanded.astype(jnp.bfloat16).reshape(KBLK, -1)


def per_device(queries, latent_cache, selected, value_weight):
    latent_width = DC + DR
    blocks_here = selected.shape[0]
    ctx_size = lax.axis_size("ctx")
    slice_width = latent_cache.shape[1] // ctx_size
    spread = lax.all_to_all(
        latent_cache.reshape(blocks_here, ctx_size, slice_width),
        "ctx",
        split_axis=1,
        concat_axis=0,
        tiled=True,
    )
    banded = spread.reshape(blocks_here * ctx_size, slice_width)
    every_choice = lax.all_gather(selected, "ctx", axis=0, tiled=True)
    clipped_all = jnp.maximum(every_choice, 0)
    pieces = banded[clipped_all].reshape(ctx_size, blocks_here, SEL, slice_width)
    fetched = lax.all_to_all(pieces, "ctx", split_axis=0, concat_axis=3, tiled=True)
    key_blocks = fetched.reshape(blocks_here, SEL * KBLK, latent_width)
    base_block = lax.axis_index("ctx") * blocks_here

    def one_block(position):
        query_rows = lax.dynamic_slice_in_dim(queries, position * KBLK, KBLK, 0)
        return attend_block(
            query_rows,
            key_blocks[position],
            selected[position],
            base_block + position,
            value_weight,
        )

    attended_here = lax.map(one_block, jnp.arange(blocks_here, dtype=jnp.int32))
    attended_here = attended_here.reshape(blocks_here * KBLK, -1)
    return lax.all_to_all(attended_here, "head", split_axis=0, concat_axis=1, tiled=True)


def solution(mesh):
    in_specs = (P("ctx", "head", None), P("ctx", None), P("ctx", None), P("head", None, None))
    out_specs = P(("ctx", "head"), None)
    return jax.shard_map(
        per_device, mesh=mesh, in_specs=in_specs, out_specs=out_specs, check_vma=False
    )
```

profile of v0, /device:TPU:25, one launch (start us, length us, event | category | flops | bytes accessed | tf_op | source)
XLA Modules:
  0.0 173.4 jit_solution(5769751596730198066)
XLA Ops:
  0.0 1.2 reshape.110
  1.2 0.9 copy.22
  2.1 17.6 %all-to-all-start = ((bf16[2,128,288]{2,0,1:T(2,128)(2,1)}), bf16[2,128,288]{2,0,1:T(2,128)(2,1)S(1)}, u32[]{:S(2)}, u32[]{:S(2)}) async-start(bf16[2,128,288]{2,0,1:T(2,128)(2,1)} %copy.22), calls=%async_computation | async-start | bytes 393216 | tf_op jit(solution)/shard_map/all_to_all | solution.py:44
  19.7 50.8 %all-gather = s32[128,2,8]{2,1,0:T(2,128)S(1)} all-gather(s32[1,2,8]{2,1,0:T(2,128)} %bitcast.70), channel_id=1, replica_groups=mesh['ctx'=128,'head'=4] {'ctx'}, dimensions={0}, use_global_device_ids=true | all-gather | bytes 8256 | tf_op jit(solution)/shard_map/all_gather | solution.py:52
  70.6 0.2 reshape.116
  70.8 0.2 reshape.111
  71.0 9.1 %gather_fusion = bf16[2048,288]{1,0:T(8,128)(2,1)} fusion(bf16[256,288]{1,0:T(8,128)(2,1)S(1)} %reshape.111, s32[2048]{0:T(1024)S(1)} %broadcast_clamp_fusion), kind=kCustom, calls=%fused_computation | custom fusion | bytes 2367488 | tf_op jit(solution)/shard_map/gather | solution.py:54
  80.1 10.4 %all-to-all-start.1 = ((bf16[128,2,8,288]{3,2,1,0:T(8,128)(2,1)}), bf16[128,2,8,288]{3,2,1,0:T(8,128)(2,1)S(1)}, u32[]{:S(2)}, u32[]{:S(2)}) async-start(bf16[128,2,8,288]{3,2,1,0:T(8,128)(2,1)} %bitcast.11), calls=%async_computation.1 | async-start | bytes 3145728 | tf_op jit(solution)/shard_map/all_to_all | solution.py:55
  90.5 4.3 %copy.25 = bf16[128,16,576]{2,0,1:T(8,128)(2,1)} copy(bf16[128,16,576]{0,2,1:T(8,128)(2,1)} %param.6) | data formatting | bytes 4718592 | tf_op jit(solution)/shard_map/while | solution.py:69
  94.8 36.2 %all-to-all-done.1 = bf16[128,2,8,288]{3,2,1,0:T(8,128)(2,1)S(1)} async-done(((bf16[128,2,8,288]{3,2,1,0:T(8,128)(2,1)}), bf16[128,2,8,288]{3,2,1,0:T(8,128)(2,1)S(1)}, u32[]{:S(2)}, u32[]{:S(2)}) %all-to-all-start.1) | async-done | bytes 1179680 | tf_op jit(solution)/shard_map/all_to_all | solution.py:55
  131.0 0.4 copy.23
  131.4 1.9 %reshape.113 = bf16[2,512,576]{2,1,0:T(8,128)(2,1)} reshape(bf16[1,2,8,128,288]{4,3,2,1,0:T(8,128)(2,1)S(1)} %copy.23) | data formatting | bytes 2359296 | tf_op jit(solution)/shard_map/reshape | solution.py:56
  133.3 1.6 copy.24
  134.9 23.8 %while.10 = (s32[]{:T(128)}, bf16[2,64,2048]{2,1,0:T(8,128)(2,1)S(1)}, s32[2]{0:T(128)S(1)}, bf16[2,512,576]{1,2,0:T(8,128)(2,1)S(1)}, s32[2,8]{1,0:T(2,128)S(1)...) while((s32[]{:T(128)}, ...), condition=%wide.region_3.4_spmd, body=%wide.region_0.3_spmd.sunk | while | flops 1278936192 | bytes 11819933 | solution.py:69
  135.0 0.6 dynamic_slice.52
  137.6 0.1 add.67
  137.7 0.1 and.23
  138.5 0.1 compare_and_fusion.2
  139.2 4.0 %fusion.43 = (f32[16,64]{1,0:T(8,128)S(1)}, f32[16,64,512]{2,1,0:T(8,128)}) fusion(pred[64,512]{1,0:T(8,128)(4,1)S(1)} %compare_and_fusion.2, bf16[128,16,576]{2,0,1:T(8,128)(2,1)} %get-tuple-element.183, s32[]{:T(128)S(6)} %select_n.23, bf16[2,512,576]{1,2,0:T(8,128)(2,1)S(1)} %get-tuple-element.180, s32[]{:T(128)S(6)} %select_n.22), kind=kOutput, calls=%fused_computation.32.clone.1 | convolution fusion | flops 606077440 | bytes 4034568 | tf_op jit(solution)/shard_map/while/body/eval_jaxpr/sub | solution.py:28
  143.2 3.3 %fusion.44 = bf16[64,16,128]{2,0,1:T(8,128)(2,1)S(1)} fusion(bf16[16,512,128]{2,1,0:T(8,128)(2,1)} %get-tuple-element.184, f32[16,64,512]{2,1,0:T(8,128)} %get-tuple-element.149, f32[16,64]{1,0:T(8,128)S(1)} %get-tuple-element.150, bf16[512,576]{0,1:T(8,128)(2,1)S(1)} %dynamic-slice_bitcast_fusion.2), kind=kOutput, calls=%fused_computation.11.clone.1 | convolution fusion | flops 672792576 | bytes 4988928 | tf_op jit(solution)/shard_map/while/body/eval_jaxpr/qhc,hcv->qhv/dot_general | solution.py:33
  146.5 0.2 copy.31
  146.7 0.1 broadcast_in_dim.53
  146.9 0.6 dynamic_slice.52
  149.5 0.1 add.67
  149.7 0.1 and.23
  150.4 0.1 compare_and_fusion.2
  151.2 4.0 %fusion.43 = (f32[16,64]{1,0:T(8,128)S(1)}, f32[16,64,512]{2,1,0:T(8,128)}) fusion(pred[64,512]{1,0:T(8,128)(4,1)S(1)} %compare_and_fusion.2, bf16[128,16,576]{2,0,1:T(8,128)(2,1)} %get-tuple-element.183, s32[]{:T(128)S(6)} %select_n.23, bf16[2,512,576]{1,2,0:T(8,128)(2,1)S(1)} %get-tuple-element.180, s32[]{:T(128)S(6)} %select_n.22), kind=kOutput, calls=%fused_computation.32.clone.1 | convolution fusion | flops 606077440 | bytes 4034568 | tf_op jit(solution)/shard_map/while/body/eval_jaxpr/sub | solution.py:28
  155.2 3.3 %fusion.44 = bf16[64,16,128]{2,0,1:T(8,128)(2,1)S(1)} fusion(bf16[16,512,128]{2,1,0:T(8,128)(2,1)} %get-tuple-element.184, f32[16,64,512]{2,1,0:T(8,128)} %get-tuple-element.149, f32[16,64]{1,0:T(8,128)S(1)} %get-tuple-element.150, bf16[512,576]{0,1:T(8,128)(2,1)S(1)} %dynamic-slice_bitcast_fusion.2), kind=kOutput, calls=%fused_computation.11.clone.1 | convolution fusion | flops 672792576 | bytes 4988928 | tf_op jit(solution)/shard_map/while/body/eval_jaxpr/qhc,hcv->qhv/dot_general | solution.py:33
  158.5 0.2 copy.31
  158.6 0.1 broadcast_in_dim.53
  158.8 13.8 %all_to_all.49 = bf16[4,32,2048]{2,1,0:T(8,128)(2,1)S(1)} all-to-all(bf16[4,32,2048]{2,1,0:T(8,128)(2,1)S(1)} %bitcast.69), channel_id=1, replica_groups=mesh['ctx'=128,'head'=4] {'head'}, dimensions={0} | all-to-all | bytes 1048576 | tf_op jit(solution)/shard_map/all_to_all | solution.py:71
  172.6 0.8 copy.29
  (23 shorter events, 0.6 us)
Async XLA Ops:
  2.1 68.7 %all-to-all-start = ((bf16[2,128,288]{2,0,1:T(2,128)(2,1)}), bf16[2,128,288]{2,0,1:T(2,128)(2,1)S(1)}, u32[]{:S(2)}, u32[]{:S(2)}) async-start(bf16[2,128,288]{2,0,1:T(2,128)(2,1)} %copy.22), calls=%async_computation | async-start | bytes 393216 | tf_op jit(solution)/shard_map/all_to_all | solution.py:44
  80.1 50.9 %all-to-all-start.1 = ((bf16[128,2,8,288]{3,2,1,0:T(8,128)(2,1)}), bf16[128,2,8,288]{3,2,1,0:T(8,128)(2,1)S(1)}, u32[]{:S(2)}, u32[]{:S(2)}) async-start(bf16[128,2,8,288]{3,2,1,0:T(8,128)(2,1)} %bitcast.11), calls=%async_computation.1 | async-start | bytes 3145728 | tf_op jit(solution)/shard_map/all_to_all | solution.py:55
  131.4 3.6 %copy-start.1 = (s32[2,8]{1,0:T(2,128)S(1)}, s32[2,8]{1,0:T(2,128)}, u32[]{:S(2)}) copy-start(s32[2,8]{1,0:T(2,128)} %param.8) | copy-start | bytes 196
  133.3 1.7 copy-start
where the time goes:
time: 174 us; the launch traced here: 173 us
  blocking collectives  64.6 us (37%)
  waiting for transfers between devices  36.2 us (21%)
  starting transfers between devices  28 us (16%)
  local copies, waits for them, and re-layouts  23 us (13%)
  matrix products  14.5 us (8%)
  loops' own time  6.64 us (4%)
    all_gather x1, blocking collectives, per_device(): every_choice = lax.all_gather(selected, 'ctx', axis=0, tiled=True)  50.8 us
    all_to_all x1, waiting for transfers between devices, per_device(): lax.all_to_all(pieces, 'ctx', split_axis=0, concat_axis=3, tiled=True)  36.2 us
    all_to_all x1, starting transfers between devices, per_device(): lax.all_to_all(latent_cache.reshape(blocks_here, ctx_size, slice_width),...  17.6 us
    all_to_all x1, blocking collectives, per_device(): lax.all_to_all(attended_here, 'head', split_axis=0, concat_axis=1, tiled=...  13.8 us
    all_to_all x1, starting transfers between devices, per_device(): lax.all_to_all(pieces, 'ctx', split_axis=0, concat_axis=3, tiled=True)  10.4 us
    gather x1, local copies, waits for them, and re-layouts, per_device(): banded[clipped_all].reshape(ctx_size, blocks_here, SEL, slice_width)  9.09 us
    sub x2, matrix products, attend_block(): powered = jnp.exp(scores - largest)  7.93 us
    another operation x1, loops' own time, per_device(): attended_here = lax.map(one_block, jnp.arange(blocks_here, dtype=jnp.int32))  6.64 us
  transfers between devices with their start and end apart: 2, of which 1 were waited for; matrix products, arithmetic and copies ran while one was open for 3% of the time, Pallas kernels for 0%

commit v1 on v0

--- a/solution.py
+++ b/solution.py
@@ -49,7 +49,9 @@
         tiled=True,
     )
     banded = spread.reshape(blocks_here * ctx_size, slice_width)
-    every_choice = lax.all_gather(selected, "ctx", axis=0, tiled=True)
+    every_choice = jnp.concatenate(
+        lax.all_to_all(jnp.stack([selected] * lax.axis_size("ctx")), "ctx", 0, 0), axis=0
+    )
     clipped_all = jnp.maximum(every_choice, 0)
     pieces = banded[clipped_all].reshape(ctx_size, blocks_here, SEL, slice_width)
     fetched = lax.all_to_all(pieces, "ctx", split_axis=0, concat_axis=3, tiled=True)

time: 174 us -> 150 us (0.86)
  blocking collectives: 64.6 us -> 13.8 us
  waiting for transfers between devices: 36.2 us -> 56.1 us
  starting transfers between devices: 28 us -> 33.8 us
    all_gather x1 -> x0, blocking collectives: 50.8 us -> none  [per_device(): every_choice = lax.all_gather(selected, 'ctx', axis=0, tiled=True)]
    all_to_all x0 -> x1, starting transfers between devices: none -> 17.6 us  [per_device(): lax.all_to_all(jnp.stack([selected] * lax.axis_size('ctx')), 'ctx', 0, 0)]
    all_to_all x1, waiting for transfers between devices: 0.01 us -> 11.5 us  [per_device(): lax.all_to_all(latent_cache.reshape(blocks_here, ctx_size, slice_width),...]
    all_to_all x1, starting transfers between devices: 17.6 us -> 7.99 us  [per_device(): lax.all_to_all(latent_cache.reshape(blocks_here, ctx_size, slice_width),...]
    all_to_all x0 -> x1, waiting for transfers between devices: none -> 8.42 us  [per_device(): lax.all_to_all(jnp.stack([selected] * lax.axis_size('ctx')), 'ctx', 0, 0)]
    all_to_all x1, starting transfers between devices: 10.4 us -> 8.16 us  [per_device(): lax.all_to_all(pieces, 'ctx', split_axis=0, concat_axis=3, tiled=True)]
  transfers between devices with their start and end apart: 2 -> 3, of which waited for: 1 -> 3; matrix products, arithmetic and copies ran while one was open for 3% -> 4% of each run, Pallas kernels for 0% -> 0%
where the time goes in v1:
time: 150 us
  waiting for transfers between devices  56.1 us (37%)
  starting transfers between devices  33.8 us (23%)
  local copies, waits for them, and re-layouts  24.3 us (16%)
  matrix products  14.5 us (10%)
  blocking collectives  13.8 us (9%)
  loops' own time  6.64 us (4%)
    all_to_all x1, waiting for transfers between devices, per_device(): lax.all_to_all(pieces, 'ctx', split_axis=0, concat_axis=3, tiled=True)  36.2 us
    all_to_all x1, starting transfers between devices, per_device(): lax.all_to_all(jnp.stack([selected] * lax.axis_size('ctx')), 'ctx', 0, 0)  17.6 us
    all_to_all x1, blocking collectives, per_device(): lax.all_to_all(attended_here, 'head', split_axis=0, concat_axis=1, tiled=...  13.8 us
    all_to_all x1, waiting for transfers between devices, per_device(): lax.all_to_all(latent_cache.reshape(blocks_here, ctx_size, slice_width),...  11.5 us
    gather x1, local copies, waits for them, and re-layouts, per_device(): banded[clipped_all].reshape(ctx_size, blocks_here, SEL, slice_width)  9.06 us
    all_to_all x1, waiting for transfers between devices, per_device(): lax.all_to_all(jnp.stack([selected] * lax.axis_size('ctx')), 'ctx', 0, 0)  8.42 us
    all_to_all x1, starting transfers between devices, per_device(): lax.all_to_all(pieces, 'ctx', split_axis=0, concat_axis=3, tiled=True)  8.16 us
    all_to_all x1, starting transfers between devices, per_device(): lax.all_to_all(latent_cache.reshape(blocks_here, ctx_size, slice_width),...  7.99 us
  transfers between devices with their start and end apart: 3, of which 3 were waited for; matrix products, arithmetic and copies ran while one was open for 4% of the time, Pallas kernels for 0%

profile of v1, /device:TPU:25, one launch (start us, length us, event | category | flops | bytes accessed | tf_op | source)
XLA Modules:
  0.0 149.6 jit_solution(8763586645227421736)
XLA Ops:
  0.0 1.4 stack.2
  1.4 17.6 %all-to-all-start.1 = ((s32[128,2,8]{2,1,0:T(2,128)}), s32[128,2,8]{2,1,0:T(2,128)S(1)}, u32[]{:S(2)}, u32[]{:S(2)}) async-start(s32[128,2,8]{2,1,0:T(2,128)} %stack.2), calls=%async_computation.1 | async-start | bytes 262144 | tf_op jit(solution)/shard_map/all_to_all | solution.py:53
  19.0 1.2 reshape.125
  20.2 0.9 copy.22
  21.1 8.4 %all-to-all-done.1 = s32[128,2,8]{2,1,0:T(2,128)S(1)} async-done(((s32[128,2,8]{2,1,0:T(2,128)}), s32[128,2,8]{2,1,0:T(2,128)S(1)}, u32[]{:S(2)}, u32[]{:S(2)}) %all-to-all-start.1) | async-done | bytes 8224 | tf_op jit(solution)/shard_map/all_to_all | solution.py:53
  29.5 8.0 %all-to-all-start = ((bf16[2,128,288]{2,0,1:T(2,128)(2,1)}), bf16[2,128,288]{2,0,1:T(2,128)(2,1)S(1)}, u32[]{:S(2)}, u32[]{:S(2)}) async-start(bf16[2,128,288]{2,0,1:T(2,128)(2,1)} %copy.22), calls=%async_computation | async-start | bytes 393216 | tf_op jit(solution)/shard_map/all_to_all | solution.py:44
  37.6 0.2 reshape.131
  37.8 11.5 %all-to-all-done = bf16[2,128,288]{2,0,1:T(2,128)(2,1)S(1)} async-done(((bf16[2,128,288]{2,0,1:T(2,128)(2,1)}), bf16[2,128,288]{2,0,1:T(2,128)(2,1)S(1)}, u32[]{:S(2)}, u32[]{:S(2)}) %all-to-all-start) | async-done | bytes 147488 | tf_op jit(solution)/shard_map/all_to_all | solution.py:44
  49.3 0.2 reshape.126
  49.5 9.1 %gather_fusion = bf16[2048,288]{1,0:T(8,128)(2,1)} fusion(bf16[256,288]{1,0:T(8,128)(2,1)S(1)} %reshape.126, s32[2048]{0:T(1024)S(1)} %broadcast_clamp_fusion), kind=kCustom, calls=%fused_computation | custom fusion | bytes 2367488 | tf_op jit(solution)/shard_map/gather | solution.py:56
  58.5 8.2 %all-to-all-start.2 = ((bf16[128,2,8,288]{3,2,1,0:T(8,128)(2,1)}), bf16[128,2,8,288]{3,2,1,0:T(8,128)(2,1)S(1)}, u32[]{:S(2)}, u32[]{:S(2)}) async-start(bf16[128,2,8,288]{3,2,1,0:T(8,128)(2,1)} %bitcast.10), calls=%async_computation.2 | async-start | bytes 3145728 | tf_op jit(solution)/shard_map/all_to_all | solution.py:57
  66.7 4.3 %copy.25 = bf16[128,16,576]{2,0,1:T(8,128)(2,1)} copy(bf16[128,16,576]{0,2,1:T(8,128)(2,1)} %param.6) | data formatting | bytes 4718592 | tf_op jit(solution)/shard_map/while | solution.py:71
  71.0 36.2 %all-to-all-done.2 = bf16[128,2,8,288]{3,2,1,0:T(8,128)(2,1)S(1)} async-done(((bf16[128,2,8,288]{3,2,1,0:T(8,128)(2,1)}), bf16[128,2,8,288]{3,2,1,0:T(8,128)(2,1)S(1)}, u32[]{:S(2)}, u32[]{:S(2)}) %all-to-all-start.2) | async-done | bytes 1179680 | tf_op jit(solution)/shard_map/all_to_all | solution.py:57
  107.2 0.4 copy.23
  107.6 1.9 %reshape.128 = bf16[2,512,576]{2,1,0:T(8,128)(2,1)} reshape(bf16[1,2,8,128,288]{4,3,2,1,0:T(8,128)(2,1)S(1)} %copy.23) | data formatting | bytes 2359296 | tf_op jit(solution)/shard_map/reshape | solution.py:58
  109.5 1.6 %copy.24 = bf16[2,512,576]{1,2,0:T(8,128)(2,1)S(1)} copy(bf16[2,512,576]{2,1,0:T(8,128)(2,1)} %reshape.128) | data formatting | bytes 2359296 | tf_op jit(solution)/shard_map/while | solution.py:71
  111.1 23.8 %while.10 = (s32[]{:T(128)}, bf16[2,64,2048]{2,1,0:T(8,128)(2,1)S(1)}, s32[2]{0:T(128)S(1)}, bf16[2,512,576]{1,2,0:T(8,128)(2,1)S(1)}, s32[2,8]{1,0:T(2,128)S(1)...) while((s32[]{:T(128)}, ...), condition=%wide.region_3.4_spmd, body=%wide.region_0.3_spmd.sunk | while | flops 1278936192 | bytes 11819933 | solution.py:71
  111.1 0.6 dynamic_slice.52
  113.9 0.1 and.23
  114.7 0.1 compare_and_fusion.2
  115.4 4.0 %fusion.43 = (f32[16,64]{1,0:T(8,128)S(1)}, f32[16,64,512]{2,1,0:T(8,128)}) fusion(pred[64,512]{1,0:T(8,128)(4,1)S(1)} %compare_and_fusion.2, bf16[128,16,576]{2,0,1:T(8,128)(2,1)} %get-tuple-element.183, s32[]{:T(128)S(6)} %select_n.23, bf16[2,512,576]{1,2,0:T(8,128)(2,1)S(1)} %get-tuple-element.180, s32[]{:T(128)S(6)} %select_n.22), kind=kOutput, calls=%fused_computation.32.clone.1 | convolution fusion | flops 606077440 | bytes 4034568 | tf_op jit(solution)/shard_map/while/body/eval_jaxpr/sub | solution.py:28
  119.4 3.3 %fusion.44 = bf16[64,16,128]{2,0,1:T(8,128)(2,1)S(1)} fusion(bf16[16,512,128]{2,1,0:T(8,128)(2,1)} %get-tuple-element.184, f32[16,64,512]{2,1,0:T(8,128)} %get-tuple-element.149, f32[16,64]{1,0:T(8,128)S(1)} %get-tuple-element.150, bf16[512,576]{0,1:T(8,128)(2,1)S(1)} %dynamic-slice_bitcast_fusion.2), kind=kOutput, calls=%fused_computation.11.clone.1 | convolution fusion | flops 672792576 | bytes 4988928 | tf_op jit(solution)/shard_map/while/body/eval_jaxpr/qhc,hcv->qhv/dot_general | solution.py:33
  122.7 0.2 copy.31
  122.9 0.1 broadcast_in_dim.50
  123.1 0.6 dynamic_slice.52
  126.6 0.1 compare_and_fusion.2
  127.4 4.0 %fusion.43 = (f32[16,64]{1,0:T(8,128)S(1)}, f32[16,64,512]{2,1,0:T(8,128)}) fusion(pred[64,512]{1,0:T(8,128)(4,1)S(1)} %compare_and_fusion.2, bf16[128,16,576]{2,0,1:T(8,128)(2,1)} %get-tuple-element.183, s32[]{:T(128)S(6)} %select_n.23, bf16[2,512,576]{1,2,0:T(8,128)(2,1)S(1)} %get-tuple-element.180, s32[]{:T(128)S(6)} %select_n.22), kind=kOutput, calls=%fused_computation.32.clone.1 | convolution fusion | flops 606077440 | bytes 4034568 | tf_op jit(solution)/shard_map/while/body/eval_jaxpr/sub | solution.py:28
  131.3 3.3 %fusion.44 = bf16[64,16,128]{2,0,1:T(8,128)(2,1)S(1)} fusion(bf16[16,512,128]{2,1,0:T(8,128)(2,1)} %get-tuple-element.184, f32[16,64,512]{2,1,0:T(8,128)} %get-tuple-element.149, f32[16,64]{1,0:T(8,128)S(1)} %get-tuple-element.150, bf16[512,576]{0,1:T(8,128)(2,1)S(1)} %dynamic-slice_bitcast_fusion.2), kind=kOutput, calls=%fused_computation.11.clone.1 | convolution fusion | flops 672792576 | bytes 4988928 | tf_op jit(solution)/shard_map/while/body/eval_jaxpr/qhc,hcv->qhv/dot_general | solution.py:33
  134.6 0.2 copy.31
  134.8 0.1 broadcast_in_dim.50
  135.0 13.8 %all_to_all.54 = bf16[4,32,2048]{2,1,0:T(8,128)(2,1)S(1)} all-to-all(bf16[4,32,2048]{2,1,0:T(8,128)(2,1)S(1)} %bitcast.68), channel_id=1, replica_groups=mesh['ctx'=128,'head'=4] {'head'}, dimensions={0} | all-to-all | bytes 1048576 | tf_op jit(solution)/shard_map/all_to_all | solution.py:73
  148.8 0.8 copy.29
  (25 shorter events, 0.8 us)
Async XLA Ops:
  1.4 28.2 %all-to-all-start.1 = ((s32[128,2,8]{2,1,0:T(2,128)}), s32[128,2,8]{2,1,0:T(2,128)S(1)}, u32[]{:S(2)}, u32[]{:S(2)}) async-start(s32[128,2,8]{2,1,0:T(2,128)} %stack.2), calls=%async_computation.1 | async-start | bytes 262144 | tf_op jit(solution)/shard_map/all_to_all | solution.py:53
  29.5 19.8 %all-to-all-start = ((bf16[2,128,288]{2,0,1:T(2,128)(2,1)}), bf16[2,128,288]{2,0,1:T(2,128)(2,1)S(1)}, u32[]{:S(2)}, u32[]{:S(2)}) async-start(bf16[2,128,288]{2,0,1:T(2,128)(2,1)} %copy.22), calls=%async_computation | async-start | bytes 393216 | tf_op jit(solution)/shard_map/all_to_all | solution.py:44
  58.5 48.7 %all-to-all-start.2 = ((bf16[128,2,8,288]{3,2,1,0:T(8,128)(2,1)}), bf16[128,2,8,288]{3,2,1,0:T(8,128)(2,1)S(1)}, u32[]{:S(2)}, u32[]{:S(2)}) async-start(bf16[128,2,8,288]{3,2,1,0:T(8,128)(2,1)} %bitcast.10), calls=%async_computation.2 | async-start | bytes 3145728 | tf_op jit(solution)/shard_map/all_to_all | solution.py:57
  107.6 3.6 %copy-start.1 = (s32[2,8]{1,0:T(2,128)S(1)}, s32[2,8]{1,0:T(2,128)}, u32[]{:S(2)}) copy-start(s32[2,8]{1,0:T(2,128)} %param.8) | copy-start | bytes 196
  109.5 1.7 %copy-start = (bf16[2,64,2048]{2,1,0:T(8,128)(2,1)S(1)}, bf16[2,64,2048]{2,1,0:T(8,128)(2,1)}, u32[]{:S(2)}) copy-start(bf16[2,64,2048]{2,1,0:T(8,128)(2,1)} %custom-call.2) | copy-start | bytes 1572868
